TPU v7x, 32 devices: a whole 2x2x4 slice. The times are simulated.
32 devices in a mesh: dp: 8 (over y, x, core), mp: 4 (over z).
Axes of the slice: x: 2, y: 2, z: 4, core: 2. Of those that a mesh axis runs over, the one named last changes fastest.
Arguments:
- patches: bfloat16 [1024, 588], P('dp'), may hold values from -6 to 6
- embed_weight: bfloat16 [6144, 588], P(('mp', 'dp')), may hold values from -0.25 to 0.25
- project_weight: bfloat16 [6144, 3, 3072], P('dp', None, 'mp'), may hold values from -0.078125 to 0.078125
- patch_counts: int32 [64], P('dp'), may hold values from 0 to 64, as said below
- segment_ids: int32 [1024], P('dp'), may hold values from -1 to 63, as said below
- targets: bfloat16 [1024, 3072], P('dp', 'mp'), may hold values from -4 to 4
Outputs:
- project_grad: float32 [6144, 3, 3072], P('dp', None, 'mp')
- loss_value: float32 [], replicated
Inputs may be any that keep to these rules, and one draw needn't show every extreme that they name: `patch_counts`: entry 8 * i + j is the number of patches of image slot j of device i along dp, a multiple of 16, 0 for an empty slot; the counts of one device add up to at most 128, and some device reaches it. `segment_ids`: the rows of device i along dp hold its images whole, slot after slot, each row carrying the id 8 * i + slot of its image, then -1 on the rows left. A device in the upper half of dp holds more rows than the device half the axis away. On each device the images that end after its row 96 cover at most 64 rows. Those rows plus all the rows of the device half the axis away come to at most 96. Both bounds are reached.
All inputs are finite; a program needn't handle non-finite values.
Results may differ from a plain program's by a relative error of at most 0.012.
The roundings to bfloat16 on the way count: a program that leaves them out, or rounds other values in their place, can miss the bound.
Values may be sent and summed in bfloat16 or wider, within the bound.
A program may use at most 128 MiB of HBM per device.

v0:
```python
import math
import jax
import jax.numpy as jnp
from jax import lax
from jax.sharding import PartitionSpec as P

HD = 128


def layer_norm(values):
    center = values - jnp.mean(values, axis=-1, keepdims=True)
    spread = jnp.mean(center * center, axis=-1, keepdims=True)
    return center * lax.rsqrt(spread + 1e-06)


def norm_grad(values, cotangent):
    return jax.vjp(layer_norm, values)[1](cotangent)[0]


def attend_block(query_raw, key_raw, value_rows, segment, target):
    inverse_root = 1.0 / math.sqrt(HD)
    query_normed = layer_norm(query_raw).astype(jnp.bfloat16)
    key_normed = layer_norm(key_raw).astype(jnp.bfloat16)
    scores = (
        jnp.einsum("qhd,khd->hqk", query_normed, key_normed, preferred_element_type=jnp.float32)
        * inverse_root
    )
    valid = segment >= 0
    allowed = (segment[:, None] == segment[None, :]) & valid[:, None]
    exponent = jnp.where(allowed[None], jnp.exp(scores), 0.0)
    denominator = jnp.sum(exponent, axis=-1, keepdims=True)
    denominator = jnp.where(valid[None, :, None], denominator, 1.0)
    weights = (exponent / denominator).astype(jnp.bfloat16)
    attended = jnp.einsum("hqk,khd->qhd", weights, value_rows, preferred_element_type=jnp.float32)
    feature_count = attended.shape[1] * attended.shape[2]
    error_rows = jnp.where(
        valid[:, None], attended.reshape(-1, feature_count) - target.astype(jnp.float32), 0.0
    )
    squared_sum = jnp.sum(error_rows * error_rows)
    return (query_normed, key_normed, weights, error_rows, squared_sum)


def attend_back(
    query_raw, key_raw, query_normed, key_normed, value_rows, weights, error_rows, patch_total
):
    inverse_root = 1.0 / math.sqrt(HD)
    out_grad = (error_rows / patch_total).astype(jnp.bfloat16).reshape(query_normed.shape)
    prob_grad = jnp.einsum("qhd,khd->hqk", out_grad, value_rows, preferred_element_type=jnp.float32)
    value_grad = jnp.einsum(
        "hqk,qhd->khd", weights, out_grad, preferred_element_type=jnp.float32
    ).astype(jnp.bfloat16)
    weight_float = weights.astype(jnp.float32)
    score_grad = (
        weight_float
        * (prob_grad - jnp.sum(prob_grad * weight_float, axis=-1, keepdims=True))
        * inverse_root
    ).astype(jnp.bfloat16)
    normed_grad_q = jnp.einsum(
        "hqk,khd->qhd", score_grad, key_normed, preferred_element_type=jnp.float32
    )
    normed_grad_k = jnp.einsum(
        "hqk,qhd->khd", score_grad, query_normed, preferred_element_type=jnp.float32
    )
    query_grad = norm_grad(query_raw, normed_grad_q).astype(jnp.bfloat16)
    key_grad = norm_grad(key_raw, normed_grad_k).astype(jnp.bfloat16)
    return jnp.stack([query_grad, key_grad, value_grad], axis=1)


def local(patches, embed_weight, project_weight, patch_counts, segment_ids, targets):
    local_total = jnp.sum(patch_counts).astype(jnp.float32)
    patch_total = lax.psum(local_total, "dp")
    row_total = patches.shape[0]
    own_features = jnp.einsum(
        "rp,cp->rc",
        patches,
        lax.all_gather(embed_weight, "dp", axis=0, tiled=True),
        preferred_element_type=jnp.float32,
    ).astype(jnp.bfloat16)
    embedded = lax.all_gather(own_features, "mp", axis=1, tiled=True)
    normed = layer_norm(embedded.astype(jnp.float32)).astype(jnp.bfloat16)
    flat_weight = project_weight.reshape(project_weight.shape[0], -1)
    section = normed
    projected = jnp.dot(
        section,
        lax.all_gather(flat_weight, "dp", axis=0, tiled=True),
        preferred_element_type=jnp.float32,
    )
    head_dev = project_weight.shape[2] // HD
    projected = projected.reshape(row_total, 3, head_dev, HD)
    query_raw = projected[:, 0]
    key_raw = projected[:, 1]
    value_rows = projected[:, 2].astype(jnp.bfloat16)
    query_normed, key_normed, weights, error_rows, squared_sum = attend_block(
        query_raw, key_raw, value_rows, segment_ids, targets
    )
    loss_value = lax.psum(squared_sum, ("dp", "mp")) / (2.0 * patch_total)
    grad_rows = attend_back(
        query_raw, key_raw, query_normed, key_normed, value_rows, weights, error_rows, patch_total
    )
    grad_rows = grad_rows.reshape(row_total, -1)
    normed_blocks = lax.all_to_all(normed, "dp", split_axis=1, concat_axis=0, tiled=True)
    section = normed_blocks
    weight_grad = lax.dot_general(
        section,
        lax.all_gather(grad_rows, "dp", axis=0, tiled=True),
        (((0,), (0,)), ((), ())),
        preferred_element_type=jnp.float32,
    )
    return (weight_grad.reshape(weight_grad.shape[0], 3, -1), loss_value)


def solution(mesh):
    in_specs = (
        P("dp", None),
        P(("mp", "dp"), None),
        P("dp", None, "mp"),
        P("dp"),
        P("dp"),
        P("dp", "mp"),
    )
    out_specs = (P("dp", None, "mp"), P())
    return jax.shard_map(local, mesh=mesh, in_specs=in_specs, out_specs=out_specs, check_vma=False)
```

profile of v0, /device:TPU:0, one launch (start us, length us, event | category | flops | bytes accessed | tf_op | source)
XLA Modules:
  0.0 322.9 jit_solution(9939542595625254220)
XLA Ops:
  7.2 0.0 copy-start
  7.2 0.0 all-gather.5.cloned.1.call-start
  7.2 0.7 all-gather.5.cloned.1.call-update
  7.9 0.0 all-gather.7.cloned.1.call-start
  8.0 31.9 %all-gather.5.cloned.1.call-done = bf16[1536,588]{1,0:T(8,128)(2,1)} async-done(((bf16[192,588]{1,0:T(8,128)(2,1)}), bf16[1536,588]{1,0:T(8,128)(2,1)}) %all-gather.5.cloned.1.call-update) | async-done | bytes 1806352 | tf_op jit(solution)/shard_map/all_gather | solution.py:76
  39.9 0.0 copy-done
  39.9 3.1 convolution_convert_fusion
  43.0 0.0 all-gather.7.cloned.1.call-update
  43.0 0.0 all-gather.9.cloned.1.call-start
  43.0 6.0 %copy.36 = bf16[768,3,768]{0,2,1:T(8,128)(2,1)} copy(bf16[768,3,768]{2,0,1:T(8,128)(2,1)} %param.8) | data formatting | bytes 7077888 | tf_op args[2]
  49.1 0.0 copy-start.6
  49.1 0.0 copy-start.4
  49.1 0.0 copy-start.5
  49.1 0.0 all-gather.9.cloned.1.call-update
  49.1 0.0 all-gather.11.cloned.1.call-start
  49.1 0.6 copy-done.6
  49.7 0.6 reduce_sum.134
  51.0 14.4 %psum.14 = f32[]{:T(128)} all-reduce(f32[]{:T(128)S(6)} %convert_element_type.58), channel_id=1, replica_groups=mesh['dp'=8,'mp'=4] {'dp'}, use_global_device_ids=true, to_apply=%region_8.9 | all-reduce | flops 1 | bytes 8 | tf_op jit(solution)/shard_map/psum | solution.py:71
  65.4 0.0 copy-done.4
  65.4 0.2 copy.41
  65.6 0.0 copy-done.5
  65.6 0.1 compare_and_fusion
  65.7 14.5 %all-gather.7.cloned.1.call-done = bf16[128,6144]{1,0:T(8,128)(2,1)} async-done(((bf16[128,1536]{1,0:T(8,128)(2,1)}), bf16[128,6144]{1,0:T(8,128)(2,1)}) %all-gather.7.cloned.1.call-update) | async-done | bytes 1572880 | tf_op jit(solution)/shard_map/all_gather | solution.py:79
  80.2 0.0 copy-start.1
  80.2 1.8 convert_reduce_fusion
  82.0 0.1 copy-done.1
  82.0 0.6 fusion.3
  82.6 0.5 fusion.4
  83.1 136.3 %all-gather.9.cloned.1.call-done = bf16[6144,2304]{0,1:T(8,128)(2,1)} async-done(((bf16[768,2304]{0,1:T(8,128)(2,1)}), bf16[6144,2304]{0,1:T(8,128)(2,1)}) %all-gather.9.cloned.1.call-update) | async-done | bytes 28311568 | tf_op jit(solution)/shard_map/all_gather | solution.py:85
  219.4 12.7 %fusion.43 = f32[128,2304]{0,1:T(8,128)S(1)} fusion(bf16[128,6144]{1,0:T(8,128)(2,1)S(1)} %fusion.4, bf16[6144,2304]{0,1:T(8,128)(2,1)} %all-gather.9.cloned.1.call-done), kind=kOutput, calls=%fused_computation.75 | convolution fusion | flops 3623878656 | bytes 31064064 | tf_op jit(solution)/shard_map/dot_general | solution.py:83
  232.1 0.1 slice_reduce_fusion
  232.2 0.1 multiply_reduce_fusion.4
  232.3 0.3 fusion.38
  232.7 0.2 fusion.28
  232.9 1.4 multiply_reduce_fusion.1
  234.2 0.3 fusion.26
  234.5 0.0 copy-start.3
  234.5 0.9 fusion.11
  235.5 1.0 multiply_reduce_fusion.3
  236.5 0.0 copy-done.3
  236.5 1.6 fusion.30
  238.1 0.0 copy-start.2
  238.2 1.3 fusion.21
  239.5 0.1 fusion.22
  239.6 0.0 copy-done.2
  239.6 0.9 pad_maximum_fusion
  240.5 0.0 all-gather.11.cloned.1.call-update
  240.5 1.2 copy.59
  241.8 3.6 %all-to-all-start = ((bf16[128,8,768]{2,0,1:T(8,128)(2,1)}), bf16[128,8,768]{2,0,1:T(8,128)(2,1)S(1)}, u32[]{:S(2)}, u32[]{:S(2)}) async-start(bf16[128,8,768]{2,0,1:T(8,128)(2,1)} %bitcast.92), calls=%async_computation | async-start | bytes 3145728 | tf_op jit(solution)/shard_map/all_to_all | solution.py:101
  246.0 60.2 %psum.15 = f32[]{:T(128)} all-reduce(f32[]{:T(128)} %get-tuple-element.10), channel_id=1, replica_groups=mesh['dp'=8,'mp'=4] {'dp','mp'}, use_global_device_ids=true, to_apply=%region_15.16 | all-reduce | flops 1 | bytes 8 | tf_op jit(solution)/shard_map/psum | solution.py:96
  306.8 0.0 all-to-all-done
  306.8 0.0 all-gather.11.cloned.1.call-done
  306.9 8.4 %fusion.44 = f32[768,3,768]{2,0,1:T(8,128)} fusion(bf16[1024,768,1]{1,0,2:T(8,128)(2,1)S(1)} %bitcast.107, bf16[3,768,1024]{2,1,0:T(8,128)(2,1)} %bitcast.108), kind=kOutput, calls=%fused_computation.76 | convolution fusion | flops 3623878656 | bytes 13369344 | tf_op jit(solution)/shard_map/dot_general | solution.py:103
  (12 shorter events, 0.1 us)
Async XLA Ops:
  7.2 32.7 %copy-start = (bf16[128,588]{0,1:T(8,128)(2,1)S(1)}, bf16[128,588]{0,1:T(8,128)(2,1)}, u32[]{:S(2)}) copy-start(bf16[128,588]{0,1:T(8,128)(2,1)} %param.6) | copy-start | bytes 451588
  7.2 32.7 %all-gather.5.cloned.1.call-start = ((), (), s32[]{:S(2)}) async-start(), calls=%async_computation.1 | async-start | bytes 2211840 | tf_op jit(solution)/shard_map/all_gather | solution.py:76
  7.9 72.3 %all-gather.7.cloned.1.call-start = ((), (), s32[]{:S(2)}) async-start(), calls=%async_computation.2 | async-start | bytes 1966080 | tf_op jit(solution)/shard_map/all_gather | solution.py:79
  43.0 176.4 %all-gather.9.cloned.1.call-start = ((), (), s32[]{:S(2)}) async-start(), calls=%async_computation.3 | async-start | bytes 31850496 | tf_op jit(solution)/shard_map/all_gather | solution.py:85
  49.1 0.7 copy-start.6
  49.1 16.3 %copy-start.4 = (bf16[128,768]{1,0:T(8,128)(2,1)S(1)}, bf16[128,768]{1,0:T(8,128)(2,1)}, u32[]{:S(2)}) copy-start(bf16[128,768]{1,0:T(8,128)(2,1)} %param.11) | copy-start | bytes 589828
  49.1 16.5 %copy-start.5 = (s32[128]{0:T(128)S(1)}, s32[128]{0:T(128)}, u32[]{:S(2)}) copy-start(s32[128]{0:T(128)} %param.10) | copy-start | bytes 1540
  49.1 257.8 %all-gather.11.cloned.1.call-start = ((), (), s32[]{:S(2)}) async-start(), calls=%async_computation.4 | async-start | bytes 5308416 | tf_op jit(solution)/shard_map/all_gather | solution.py:105
  80.2 1.9 copy-start.1
  234.5 2.0 copy-start.3
  238.1 1.4 copy-start.2
  241.8 65.1 %all-to-all-start = ((bf16[128,8,768]{2,0,1:T(8,128)(2,1)}), bf16[128,8,768]{2,0,1:T(8,128)(2,1)S(1)}, u32[]{:S(2)}, u32[]{:S(2)}) async-start(bf16[128,8,768]{2,0,1:T(8,128)(2,1)} %bitcast.92), calls=%async_computation | async-start | bytes 3145728 | tf_op jit(solution)/shard_map/all_to_all | solution.py:101
Sparse Core Ops, SparseCore 0:
  9.9 29.9 all-gather.4
  43.1 37.0 all-gather.6
  82.7 136.7 all-gather.8
  240.6 52.0 all-gather.10
where the time goes:
time: 324 us; the launch traced here: 323 us
  waiting for transfers between devices  183 us (56%)
  blocking collectives  74.6 us (23%)
  matrix products  28.5 us (9%)
  between operations  17.1 us (5%)
  local copies, waits for them, and re-layouts  8.09 us (2%)
  other arithmetic  7.53 us (2%)
  starting transfers between devices  3.74 us (1%)
    all_gather x1, waiting for transfers between devices, local(): lax.all_gather(flat_weight, 'dp', axis=0, tiled=True)  136 us
    psum x1, blocking collectives, local(): loss_value = lax.psum(squared_sum, ('dp', 'mp')) / (2.0 * patch_total)  60.2 us
    all_gather x1, waiting for transfers between devices, local(): lax.all_gather(embed_weight, 'dp', axis=0, tiled=True)  31.9 us
    all_gather x1, waiting for transfers between devices, local(): embedded = lax.all_gather(own_features, 'mp', axis=1, tiled=True)  14.5 us
    psum x1, blocking collectives, local(): patch_total = lax.psum(local_total, 'dp')  14.4 us
    dot_general x1, matrix products, local(): jnp.dot(section, lax.all_gather(flat_weight, 'dp', axis=0, tiled=True), p...  12.7 us
    dot_general x1, matrix products, local(): lax.dot_general(section, lax.all_gather(grad_rows, 'dp', axis=0, tiled=Tr...  8.4 us
    unnamed x16, local copies, waits for them, and re-layouts  6.84 us
  transfers between devices with their start and end apart: 5, of which 3 were waited for; matrix products, arithmetic and copies ran while one was open for 3% of the time, Pallas kernels for 0%

commit v1 on v0

--- a/solution.py
+++ b/solution.py
@@ -5,6 +5,17 @@
 from jax.sharding import PartitionSpec as P
 
 HD = 128
+
+
+def ring_gather(shard, axis, dim):
+    ways = lax.axis_size(axis)
+    pieces = [shard]
+    for far in range(1, ways):
+        pieces.append(
+            lax.ppermute(pieces[far - 1], axis, [(d, (d - 1) % ways) for d in range(ways)])
+        )
+    line = jnp.concatenate(pieces, axis=dim)
+    return jnp.roll(line, lax.axis_index(axis) * shard.shape[dim], axis=dim)
 
 
 def layer_norm(values):
@@ -81,9 +92,7 @@
     flat_weight = project_weight.reshape(project_weight.shape[0], -1)
     section = normed
     projected = jnp.dot(
-        section,
-        lax.all_gather(flat_weight, "dp", axis=0, tiled=True),
-        preferred_element_type=jnp.float32,
+        section, ring_gather(flat_weight, "dp", 0), preferred_element_type=jnp.float32
     )
     head_dev = project_weight.shape[2] // HD
     projected = projected.reshape(row_total, 3, head_dev, HD)

time: 324 us -> 475 us (1.47)
  local copies, waits for them, and re-layouts: 8.09 us -> 63.4 us
  waiting for transfers between devices: 183 us -> 231 us
  blocking collectives: 74.6 us -> 97.8 us
  starting transfers between devices: 3.74 us -> 21.9 us
    ppermute x0 -> x7, waiting for transfers between devices: none -> 218 us  [ring_gather(): lax.ppermute(pieces[far - 1], axis, [(d, (d - 1) % ways) for d in range(w...]
    all_gather x1 -> x0, waiting for transfers between devices: 136 us -> none  [local(): lax.all_gather(flat_weight, 'dp', axis=0, tiled=True)]
    unnamed x16 -> x45, local copies, waits for them, and re-layouts: 6.84 us -> 60 us
    psum x1, blocking collectives: 14.4 us -> 37.5 us  [local(): patch_total = lax.psum(local_total, 'dp')]
    all_gather x1, waiting for transfers between devices: 31.9 us -> 13.4 us  [local(): lax.all_gather(embed_weight, 'dp', axis=0, tiled=True)]
    ppermute x0 -> x7, starting transfers between devices: none -> 17.7 us  [ring_gather(): lax.ppermute(pieces[far - 1], axis, [(d, (d - 1) % ways) for d in range(w...]
    all_gather x1, waiting for transfers between devices: 14.5 us -> 0.01 us  [local(): embedded = lax.all_gather(own_features, 'mp', axis=1, tiled=True)]
  transfers between devices with their start and end apart: 5 -> 11, of which waited for: 3 -> 7; matrix products, arithmetic and copies ran while one was open for 3% -> 7% of each run, Pallas kernels for 0% -> 0%
where the time goes in v1:
time: 475 us; the launch traced here: 474 us
  waiting for transfers between devices  231 us (49%)
  blocking collectives  97.8 us (21%)
  local copies, waits for them, and re-layouts  63.4 us (13%)
  matrix products  31.4 us (7%)
  starting transfers between devices  21.9 us (5%)
  between operations  17.1 us (4%)
  other arithmetic  11.2 us (2%)
    ppermute x7, waiting for transfers between devices, ring_gather(): lax.ppermute(pieces[far - 1], axis, [(d, (d - 1) % ways) for d in range(w...  218 us
    psum x1, blocking collectives, local(): loss_value = lax.psum(squared_sum, ('dp', 'mp')) / (2.0 * patch_total)  60.3 us
    unnamed x45, local copies, waits for them, and re-layouts  60 us
    psum x1, blocking collectives, local(): patch_total = lax.psum(local_total, 'dp')  37.5 us
    ppermute x7, starting transfers between devices, ring_gather(): lax.ppermute(pieces[far - 1], axis, [(d, (d - 1) % ways) for d in range(w...  17.7 us
    dot_general x1, matrix products, local(): jnp.dot(section, ring_gather(flat_weight, 'dp', 0), preferred_element_typ...  15.6 us
    all_gather x1, waiting for transfers between devices, local(): lax.all_gather(embed_weight, 'dp', axis=0, tiled=True)  13.4 us
  transfers between devices with their start and end apart: 11, of which 7 were waited for; matrix products, arithmetic and copies ran while one was open for 7% of the time, Pallas kernels for 0%

profile of v1, /device:TPU:0, one launch (start us, length us, event | category | flops | bytes accessed | tf_op | source)
XLA Modules:
  0.0 474.1 jit_solution(7020632375678065910)
XLA Ops:
  7.2 0.0 all-gather.4.cloned.1.call-start
  7.2 6.1 %copy.36 = bf16[768,3,768]{0,2,1:T(8,128)(2,1)} copy(bf16[768,3,768]{2,0,1:T(8,128)(2,1)} %param.8) | data formatting | bytes 7077888 | tf_op args[2]
  13.4 3.4 collective-permute-start
  16.7 39.3 %collective-permute-done = bf16[768,2304]{0,1:T(8,128)(2,1)S(1)} collective-permute-done((bf16[768,2304]{0,1:T(8,128)(2,1)}, bf16[768,2304]{0,1:T(8,128)(2,1)S(1)}, u32[]{:S(2)}, u32[]{:S(2)}) %collective-permute-start) | collective-permute-done | bytes 3538976 | tf_op jit(solution)/shard_map/ppermute | solution.py:15
  56.0 1.8 copy-done.3
  57.8 2.7 collective-permute-start.1
  60.5 39.0 %collective-permute-done.1 = bf16[768,2304]{0,1:T(8,128)(2,1)S(1)} collective-permute-done((bf16[768,2304]{0,1:T(8,128)(2,1)S(1)}, bf16[768,2304]{0,1:T(8,128)(2,1)S(1)}, u32[]{:S(2)}, u32[]{:S(2)}) %collective-permute-start.1) | collective-permute-done | bytes 3538976 | tf_op jit(solution)/shard_map/ppermute | solution.py:15
  99.5 1.8 copy-done.6
  101.3 2.8 collective-permute-start.2
  104.1 39.0 %collective-permute-done.2 = bf16[768,2304]{0,1:T(8,128)(2,1)S(1)} collective-permute-done((bf16[768,2304]{0,1:T(8,128)(2,1)S(1)}, bf16[768,2304]{0,1:T(8,128)(2,1)S(1)}, u32[]{:S(2)}, u32[]{:S(2)}) %collective-permute-start.2) | collective-permute-done | bytes 3538976 | tf_op jit(solution)/shard_map/ppermute | solution.py:15
  143.1 1.8 copy-done.8
  145.0 2.8 collective-permute-start.3
  147.8 39.0 %collective-permute-done.3 = bf16[768,2304]{0,1:T(8,128)(2,1)} collective-permute-done((bf16[768,2304]{0,1:T(8,128)(2,1)S(1)}, bf16[768,2304]{0,1:T(8,128)(2,1)}, u32[]{:S(2)}, u32[]{:S(2)}) %collective-permute-start.3) | collective-permute-done | bytes 3538976 | tf_op jit(solution)/shard_map/ppermute | solution.py:15
  186.8 2.9 collective-permute-start.4
  189.7 0.0 all-gather.6.cloned.1.call-start
  189.7 41.9 %collective-permute-done.4 = bf16[768,2304]{0,1:T(8,128)(2,1)} collective-permute-done((bf16[768,2304]{0,1:T(8,128)(2,1)}, bf16[768,2304]{0,1:T(8,128)(2,1)}, u32[]{:S(2)}, u32[]{:S(2)}) %collective-permute-start.4) | collective-permute-done | bytes 3538976 | tf_op jit(solution)/shard_map/ppermute | solution.py:15
  231.7 2.9 collective-permute-start.5
  234.5 13.4 %all-gather.4.cloned.1.call-done = bf16[1536,588]{1,0:T(8,128)(2,1)} async-done(((bf16[192,588]{1,0:T(8,128)(2,1)}), bf16[1536,588]{1,0:T(8,128)(2,1)}) %all-gather.4.cloned.1.call-update) | async-done | bytes 1806352 | tf_op jit(solution)/shard_map/all_gather | solution.py:87
  248.0 3.1 convolution_convert_fusion
  251.1 0.0 all-gather.8.cloned.1.call-start
  251.1 0.6 reduce_sum.134
  252.4 37.5 %psum.14 = f32[]{:T(128)} all-reduce(f32[]{:T(128)S(6)} %convert_element_type.58), channel_id=1, replica_groups=mesh['dp'=8,'mp'=4] {'dp'}, use_global_device_ids=true, to_apply=%region_8.9 | all-reduce | flops 1 | bytes 8 | tf_op jit(solution)/shard_map/psum | solution.py:82
  289.9 0.2 copy.41
  290.1 0.1 compare_and_fusion
  290.2 4.2 constant_dynamic-update-slice_fusion.15
  294.4 2.1 constant_dynamic-update-slice_fusion.14
  296.5 1.8 convert_reduce_fusion
  298.3 2.0 fusion.5
  300.3 0.2 collective-permute-start.6
  300.6 1.9 fusion.6
  302.5 2.2 constant_dynamic-update-slice_fusion.13
  304.7 1.1 copy-done.9
  305.8 2.1 constant_dynamic-update-slice_fusion.12
  307.9 4.2 constant_dynamic-update-slice_fusion.11
  312.1 4.2 constant_dynamic-update-slice_fusion.10
  316.3 4.1 constant_dynamic-update-slice_fusion.9
  320.4 19.5 %collective-permute-done.6 = bf16[768,2304]{0,1:T(8,128)(2,1)S(1)} collective-permute-done((bf16[768,2304]{0,1:T(8,128)(2,1)}, bf16[768,2304]{0,1:T(8,128)(2,1)S(1)}, u32[]{:S(2)}, u32[]{:S(2)}) %collective-permute-start.6) | collective-permute-done | bytes 3538976 | tf_op jit(solution)/shard_map/ppermute | solution.py:15
  339.9 2.1 constant_dynamic-update-slice_fusion.8
  342.0 2.1 constant_dynamic-update-slice_fusion.7
  344.1 1.2 copy-done.5
  345.3 2.1 constant_dynamic-update-slice_fusion.6
  347.4 2.1 constant_dynamic-update-slice_fusion.5
  349.5 2.2 constant_dynamic-update-slice_fusion.4
  351.6 4.0 constant_dynamic-update-slice_fusion.3
  355.7 4.1 constant_dynamic-update-slice_fusion.2
  359.8 4.2 constant_dynamic-update-slice_fusion.1
  363.9 2.2 constant_dynamic-update-slice_fusion
  366.1 15.6 %fusion.1 = f32[128,2304]{0,1:T(8,128)S(1)} fusion(bf16[128,6144]{1,0:T(8,128)(2,1)S(1)} %fusion.6, bf16[12288,2304]{0,1:T(8,128)(2,1)} %constant_dynamic-update-slice_fusion, s32[]{:T(128)S(6)} %select_n.31), kind=kOutput, calls=%fused_computation.1 | convolution fusion | flops 3623878656 | bytes 31064068 | tf_op jit(solution)/shard_map/dot_general | solution.py:94
  381.7 0.1 slice_reduce_fusion
  381.8 0.1 multiply_reduce_fusion.4
  381.9 0.3 fusion.41
  382.3 0.2 fusion.30
  382.5 1.4 multiply_reduce_fusion.1
  383.8 0.3 fusion.28
  384.1 0.9 fusion.13
  385.1 1.0 multiply_reduce_fusion.3
  386.1 1.6 fusion.32
  387.8 1.2 fusion.23
  389.0 0.1 fusion.24
  389.1 1.8 pad_maximum_fusion
  391.0 1.2 copy.59
  392.2 4.1 all-to-all-start
  397.0 60.3 %psum.15 = f32[]{:T(128)} all-reduce(f32[]{:T(128)} %get-tuple-element.10), channel_id=1, replica_groups=mesh['dp'=8,'mp'=4] {'dp','mp'}, use_global_device_ids=true, to_apply=%region_15.16 | all-reduce | flops 1 | bytes 8 | tf_op jit(solution)/shard_map/psum | solution.py:105
  458.0 8.4 %fusion.46 = f32[768,3,768]{2,0,1:T(8,128)} fusion(bf16[1024,768,1]{1,0,2:T(8,128)(2,1)S(1)} %bitcast.108, bf16[3,768,1024]{2,1,0:T(8,128)(2,1)} %bitcast.109), kind=kOutput, calls=%fused_computation.94 | convolution fusion | flops 3623878656 | bytes 13369344 | tf_op jit(solution)/shard_map/dot_general | solution.py:112
  (42 shorter events, 0.2 us)
Async XLA Ops:
  7.2 240.8 %copy-start = (bf16[128,588]{0,1:T(8,128)(2,1)S(1)}, bf16[128,588]{0,1:T(8,128)(2,1)}, u32[]{:S(2)}) copy-start(bf16[128,588]{0,1:T(8,128)(2,1)} %param.6) | copy-start | bytes 451588
  7.2 243.9 %copy-start.13 = (s32[8]{0:T(128)S(1)}, s32[8]{0:T(128)}, u32[]{:S(2)}) copy-start(s32[8]{0:T(128)} %param.9) | copy-start | bytes 100
  7.2 282.7 %copy-start.11 = (bf16[128,768]{1,0:T(8,128)(2,1)S(1)}, bf16[128,768]{1,0:T(8,128)(2,1)}, u32[]{:S(2)}) copy-start(bf16[128,768]{1,0:T(8,128)(2,1)} %param.11) | copy-start | bytes 589828
  7.2 240.8 %all-gather.4.cloned.1.call-start = ((), (), s32[]{:S(2)}) async-start(), calls=%async_computation.1 | async-start | bytes 2211840 | tf_op jit(solution)/shard_map/all_gather | solution.py:87
  13.4 276.7 %copy-start.12 = (s32[128]{0:T(128)S(1)}, s32[128]{0:T(128)}, u32[]{:S(2)}) copy-start(s32[128]{0:T(128)} %param.10) | copy-start | bytes 1540
  13.4 42.7 %collective-permute-start = (bf16[768,2304]{0,1:T(8,128)(2,1)}, bf16[768,2304]{0,1:T(8,128)(2,1)S(1)}, u32[]{:S(2)}, u32[]{:S(2)}) collective-permute-start(bf16[768,2304]{0,1:T(8,128)(2,1)} %bitcast.92), channel_id=1, source_target_pairs={{0,28},{4,0},{8,4},{12,8},{16,12},{20,16},{24,20},{28,24},{1,29},{... | collective-permute-start | bytes 10616840 | tf_op jit(solution)/shard_map/ppermute | solution.py:15
  56.0 1.8 copy-start.3
  57.8 41.7 %collective-permute-start.1 = (bf16[768,2304]{0,1:T(8,128)(2,1)S(1)}, bf16[768,2304]{0,1:T(8,128)(2,1)S(1)}, u32[]{:S(2)}, u32[]{:S(2)}) collective-permute-start(bf16[768,2304]{0,1:T(8,128)(2,1)S(1)} %collective-permute-done), channel_id=1, source_target_pairs={{0,28},{4,0},{8,4},{12,8},{16,12},{20,16},{24,20},{28,24},{1,29},{... | collective-permute-start | bytes 10616840 | tf_op jit(solution)/shard_map/ppermute | solution.py:15
  99.5 1.8 copy-start.6
  101.3 41.8 %collective-permute-start.2 = (bf16[768,2304]{0,1:T(8,128)(2,1)S(1)}, bf16[768,2304]{0,1:T(8,128)(2,1)S(1)}, u32[]{:S(2)}, u32[]{:S(2)}) collective-permute-start(bf16[768,2304]{0,1:T(8,128)(2,1)S(1)} %collective-permute-done.1), channel_id=1, source_target_pairs={{0,28},{4,0},{8,4},{12,8},{16,12},{20,16},{24,20},{28,24},{1,29},{... | collective-permute-start | bytes 10616840 | tf_op jit(solution)/shard_map/ppermute | solution.py:15
  143.1 1.8 copy-start.8
  145.0 41.8 %collective-permute-start.3 = (bf16[768,2304]{0,1:T(8,128)(2,1)S(1)}, bf16[768,2304]{0,1:T(8,128)(2,1)}, u32[]{:S(2)}, u32[]{:S(2)}) collective-permute-start(bf16[768,2304]{0,1:T(8,128)(2,1)S(1)} %collective-permute-done.2), channel_id=1, source_target_pairs={{0,28},{4,0},{8,4},{12,8},{16,12},{20,16},{24,20},{28,24},{1,29},{... | collective-permute-start | bytes 10616840 | tf_op jit(solution)/shard_map/ppermute | solution.py:15
  186.8 44.9 %collective-permute-start.4 = (bf16[768,2304]{0,1:T(8,128)(2,1)}, bf16[768,2304]{0,1:T(8,128)(2,1)}, u32[]{:S(2)}, u32[]{:S(2)}) collective-permute-start(bf16[768,2304]{0,1:T(8,128)(2,1)} %collective-permute-done.3), channel_id=1, source_target_pairs={{0,28},{4,0},{8,4},{12,8},{16,12},{20,16},{24,20},{28,24},{1,29},{... | collective-permute-start | bytes 10616840 | tf_op jit(solution)/shard_map/ppermute | solution.py:15
  189.7 106.8 %all-gather.6.cloned.1.call-start = ((), (), s32[]{:S(2)}) async-start(), calls=%async_computation.2 | async-start | bytes 1966080 | tf_op jit(solution)/shard_map/all_gather | solution.py:90
  231.7 68.6 %collective-permute-start.5 = (bf16[768,2304]{0,1:T(8,128)(2,1)}, bf16[768,2304]{0,1:T(8,128)(2,1)}, u32[]{:S(2)}, u32[]{:S(2)}) collective-permute-start(bf16[768,2304]{0,1:T(8,128)(2,1)} %collective-permute-done.4), channel_id=1, source_target_pairs={{0,28},{4,0},{8,4},{12,8},{16,12},{20,16},{24,20},{28,24},{1,29},{... | collective-permute-start | bytes 10616840 | tf_op jit(solution)/shard_map/ppermute | solution.py:15
  251.1 206.9 %all-gather.8.cloned.1.call-start = ((), (), s32[]{:S(2)}) async-start(), calls=%async_computation.3 | async-start | bytes 5308416 | tf_op jit(solution)/shard_map/all_gather | solution.py:114
  290.2 4.2 copy-start.4
  296.5 6.0 %copy-start.7 = (bf16[768,2304]{0,1:T(8,128)(2,1)S(1)}, bf16[768,2304]{0,1:T(8,128)(2,1)}, u32[]{:S(2)}) copy-start(bf16[768,2304]{0,1:T(8,128)(2,1)} %copy-done.6) | copy-start | bytes 10616836
  300.3 39.6 %collective-permute-start.6 = (bf16[768,2304]{0,1:T(8,128)(2,1)}, bf16[768,2304]{0,1:T(8,128)(2,1)S(1)}, u32[]{:S(2)}, u32[]{:S(2)}) collective-permute-start(bf16[768,2304]{0,1:T(8,128)(2,1)} %collective-permute-done.5), channel_id=1, source_target_pairs={{0,28},{4,0},{8,4},{12,8},{16,12},{20,16},{24,20},{28,24},{1,29},{... | collective-permute-start | bytes 10616840 | tf_op jit(solution)/shard_map/ppermute | solution.py:15
  302.5 3.3 copy-start.9
  320.4 21.6 %copy-start.2 = (bf16[768,3,768]{0,2,1:T(8,128)(2,1)S(1)}, bf16[768,3,768]{0,2,1:T(8,128)(2,1)}, u32[]{:S(2)}) copy-start(bf16[768,3,768]{0,2,1:T(8,128)(2,1)} %copy.36) | copy-start | bytes 10616836
  342.0 3.3 copy-start.5
  384.1 2.0 copy-start.10
  392.2 65.7 %all-to-all-start = ((bf16[128,8,768]{2,0,1:T(8,128)(2,1)}), bf16[128,8,768]{2,0,1:T(8,128)(2,1)S(1)}, u32[]{:S(2)}, u32[]{:S(2)}) async-start(bf16[128,8,768]{2,0,1:T(8,128)(2,1)} %bitcast.91), calls=%async_computation | async-start | bytes 3145728 | tf_op jit(solution)/shard_map/all_to_all | solution.py:110
  458.0 8.4 %copy-start.1 = (bf16[128,588]{0,1:T(8,128)(2,1)S(1)}, bf16[128,588]{0,1:T(8,128)(2,1)}, u32[]{:S(2)}) copy-start(bf16[128,588]{0,1:T(8,128)(2,1)} %param.6) | copy-start | bytes 451588
Sparse Core Ops, SparseCore 0:
  189.8 58.1 all-gather.3
  251.2 37.0 all-gather.5
  391.1 52.7 all-gather.7
